TPU v7x, 256 devices: a whole 4x4x8 slice. The times are simulated.
256 devices in a mesh: vocab: 256 (over z, x, y, core).
Axes of the slice: x: 4, y: 4, z: 8, core: 2. Of those that a mesh axis runs over, the one named last changes fastest.
Arguments:
- hidden: bfloat16 [4096, 2560], P('vocab'), may hold values from -3 to 3
- norm_gain: float32 [2560], replicated, may hold values from 0.1 to 1.9
- head: bfloat16 [2560, 73728], P(None, 'vocab'), may hold values from -50 to 50
- token_ids: int32 [4096], P('vocab'), may hold values from 0 to 73447
- req_len: int32 [512], replicated, may hold values from 1 to 8, as said below
- req_owner: int32 [512], replicated, may hold values from 0 to 255, as said below
Outputs:
- logprob: float32 [4096], P('vocab')
- entropy: float32 [4096], P('vocab')
Inputs may be any that keep to these rules, and one draw needn't show every extreme that they name: `req_len`: each device owns exactly 2 requests; the lengths of one device's requests sum to at most 16, and to exactly 16 on some device. `req_owner`: each device index appears exactly 2 times.
All inputs are finite; a program needn't handle non-finite values.
Results may differ from a plain program's by a relative error of at most 0.0037.
Values may be sent and summed in bfloat16 or wider, within the bound.
A program may use at most 128 MiB of HBM per device.

v0:
```python
import jax
import jax.numpy as jnp
from jax import lax
from jax.sharding import PartitionSpec as P

VOCAB_REAL = 73448
EPS = 1e-05
NEG = -1e30


def slice_stats(rows, chosen, head, col_index, real_cols):
    logits = jnp.dot(rows, head, preferred_element_type=jnp.float32) / 10.0
    logits = jnp.where(real_cols[None, :], logits, NEG)
    rowmax = jnp.max(logits, axis=1)
    expo = jnp.where(real_cols[None, :], jnp.exp(logits - rowmax[:, None]), 0.0)
    total = jnp.sum(expo, axis=1)
    weighted = jnp.sum(jnp.where(real_cols[None, :], expo * logits, 0.0), axis=1)
    picked = jnp.sum(jnp.where(col_index[None, :] == chosen[:, None], logits, 0.0), axis=1)
    return (rowmax, total, weighted, picked)


def body(hidden, norm_gain, head, token_ids, req_len, req_owner):
    local_rows = hidden.shape[0]
    columns = head.shape[1]
    me = lax.axis_index("vocab")
    values = hidden.astype(jnp.float32)
    scale = lax.rsqrt(jnp.mean(values * values, axis=-1, keepdims=True) + EPS)
    normed = (values * scale * norm_gain[None, :]).astype(jnp.bfloat16)
    col_index = me * columns + jnp.arange(columns, dtype=jnp.int32)
    real_cols = col_index < VOCAB_REAL
    all_rows, all_ids = (
        lax.all_gather(normed, "vocab", axis=0, tiled=True),
        lax.all_gather(token_ids, "vocab", axis=0, tiled=True),
    )
    stats = slice_stats(all_rows, all_ids, head, col_index, real_cols)
    rowmax, total, weighted, picked = stats

    def own_part(whole):
        return lax.dynamic_slice_in_dim(whole, me * local_rows, local_rows)

    top_full = lax.pmax(rowmax, "vocab")
    factor = jnp.exp(rowmax - top_full)
    sums = lax.psum((total * factor, weighted * factor, picked), "vocab")
    total_all, weighted_all, picked_all = [own_part(item) for item in sums]
    top = own_part(top_full)
    load = jnp.sum(jnp.where(req_owner == me, req_len, 0))
    live = jnp.arange(local_rows, dtype=jnp.int32) < load
    log_total = jnp.log(total_all)
    logprob = jnp.where(live, picked_all - top - log_total, 0.0)
    entropy = jnp.where(live, top + log_total - weighted_all / total_all, 0.0)
    return (logprob, entropy)


def solution(mesh):
    placed = (P("vocab", None), P(), P(None, "vocab"), P("vocab"), P(), P())
    return jax.shard_map(
        body, mesh=mesh, in_specs=placed, out_specs=(P("vocab"), P("vocab")), check_vma=False
    )
```

profile of v0, /device:TPU:1, one launch (start us, length us, event | category | flops | bytes accessed | tf_op | source)
XLA Modules:
  0.0 319.0 jit_solution(3615898307131070533)
XLA Ops:
  7.2 0.0 copy-start
  7.2 0.0 all-gather.2.cloned.1.call-start
  7.2 1.1 fusion.2
  8.4 1.6 fusion.4
  10.0 0.0 all-gather.2.cloned.1.call-update
  10.0 0.9 dynamic-update-slice
  10.9 82.1 %all-reduce = s32[4096]{0:T(1024)S(1)} all-reduce(s32[4096]{0:T(1024)S(1)} %dynamic-update-slice), channel_id=1, replica_groups=mesh['vocab'=256] {'vocab'}, use_global_device_ids=true, to_apply=%add | all-reduce | flops 4096 | bytes 32768
  93.0 1.4 select_reduce_fusion.2
  94.4 52.5 %all-gather.2.cloned.1.call-done = bf16[4096,2560]{1,0:T(8,128)(2,1)} async-done(((bf16[16,2560]{1,0:T(8,128)(2,1)}), bf16[4096,2560]{1,0:T(8,128)(2,1)}) %all-gather.2.cloned.1.call-update) | async-done | bytes 20971536 | tf_op jit(solution)/shard_map/all_gather | solution.py:32
  146.8 0.0 copy-done
  146.8 12.0 %fusion.7 = (f32[4096]{0:T(1024)S(1)}, f32[4096,288]{0,1:T(8,128)}) fusion(bf16[4096,2560]{1,0:T(8,128)(2,1)} %all-gather.2.cloned.1.call-done, bf16[2560,288]{0,1:T(8,128)(2,1)S(1)} %copy-done, pred[288]{0:T(512)(128)(4,1)S(1)} %broadcast_compare_fusion), kind=kOutput, calls=%fused_computation.20 | convolution fusion | flops 6043332608 | bytes 27181344 | tf_op jit(solution)/shard_map/dot_general | solution.py:12
  158.9 74.6 %pmax.7 = f32[4096]{0:T(1024)S(1)} all-reduce(f32[4096]{0:T(1024)S(1)} %get-tuple-element.12), channel_id=1, replica_groups=mesh['vocab'=256] {'vocab'}, use_global_device_ids=true, to_apply=%region_5.6 | all-reduce | flops 4096 | bytes 32768 | tf_op jit(solution)/shard_map/pmax | solution.py:41
  233.5 3.7 %select_reduce_fusion = (f32[4096]{0:T(1024)S(1)}, f32[4096]{0:T(1024)S(1)}, f32[4096]{0:T(1024)S(1)}) fusion(f32[4096,288]{0,1:T(8,128)} %get-tuple-element.13, f32[4096]{0:T(1024)S(1)} %get-tuple-element.12, pred[288]{0:T(512)(128)(4,1)S(1)} %broadcast_compare_fusion, s32[4096]{0:T(1024)S(1)} %all-reduce, s32[288]{0:T(512)S(1)} %iota_add_fusion), kind=kLoop, calls=%fused_computation.2 | loop fusion | flops 10604544 | bytes 4801952 | tf_op jit(solution)/shard_map/reduce_sum | solution.py:17
  237.2 73.8 %all-reduce.1 = (f32[4096]{0:T(1024)S(1)}, f32[4096]{0:T(1024)S(1)}, f32[4096]{0:T(1024)S(1)}) all-reduce(f32[4096]{0:T(1024)S(1)} %get-tuple-element.4, f32[4096]{0:T(1024)S(1)} %get-tuple-element.11, f32[4096]{0:T(1024)S(1)} %get-tuple-element.10), channel_id=1, replica_groups=mesh['vocab'=256] {'vocab'}, use_global_device_ids=true, to_apply=%region_3.4 | all-reduce | flops 12288 | bytes 98304 | tf_op jit(solution)/shard_map/psum | solution.py:43
  311.0 1.2 compare_select_fusion
  (5 shorter events, 0.0 us)
Async XLA Ops:
  7.2 139.7 %copy-start = (bf16[2560,288]{0,1:T(8,128)(2,1)S(1)}, bf16[2560,288]{0,1:T(8,128)(2,1)}, u32[]{:S(2)}) copy-start(bf16[2560,288]{0,1:T(8,128)(2,1)} %param.8) | copy-start | bytes 4423684
  7.2 139.7 %all-gather.2.cloned.1.call-start = ((), (), s32[]{:S(2)}) async-start(), calls=%async_computation | async-start | bytes 21053440 | tf_op jit(solution)/shard_map/all_gather | solution.py:32
Sparse Core Ops, SparseCore 0:
  11.6 135.2 all-gather.1
where the time goes:
time: 320 us; the launch traced here: 319 us
  blocking collectives  230 us (72%)
  waiting for transfers between devices  52.5 us (16%)
  between operations  14.1 us (4%)
  matrix products  12 us (4%)
  other arithmetic  9.06 us (3%)
    unnamed x1, blocking collectives  82.1 us
    pmax x1, blocking collectives, body(): top_full = lax.pmax(rowmax, 'vocab')  74.6 us
    psum x1, blocking collectives, body(): sums = lax.psum((total * factor, weighted * factor, picked), 'vocab')  73.8 us
    all_gather x1, waiting for transfers between devices, body(): lax.all_gather(normed, 'vocab', axis=0, tiled=True)  52.5 us
    dot_general x1, matrix products, slice_stats(): logits = jnp.dot(rows, head, preferred_element_type=jnp.float32) / 10.0  12 us
  transfers between devices with their start and end apart: 1, of which 1 were waited for; matrix products, arithmetic and copies ran while one was open for 1% of the time, Pallas kernels for 0%

commit v1 on v0

--- a/solution.py
+++ b/solution.py
@@ -29,7 +29,9 @@
     col_index = me * columns + jnp.arange(columns, dtype=jnp.int32)
     real_cols = col_index < VOCAB_REAL
     all_rows, all_ids = (
-        lax.all_gather(normed, "vocab", axis=0, tiled=True),
+        jnp.concatenate(
+            lax.all_to_all(jnp.stack([normed] * lax.axis_size("vocab")), "vocab", 0, 0), axis=0
+        ),
         lax.all_gather(token_ids, "vocab", axis=0, tiled=True),
     )
     stats = slice_stats(all_rows, all_ids, head, col_index, real_cols)

time: 320 us -> 691 us (2.16)
  blocking collectives: 230 us -> 645 us
  waiting for transfers between devices: 52.5 us -> 0.01 us
  starting transfers between devices: 0.04 us -> 16.5 us
  between operations: 14.1 us -> 0.71 us
    unnamed x1, blocking collectives: 82.1 us -> 498 us
    all_gather x1 -> x0, waiting for transfers between devices: 52.5 us -> none  [body(): lax.all_gather(normed, 'vocab', axis=0, tiled=True)]
    all_to_all x0 -> x1, starting transfers between devices: none -> 16.5 us  [body(): lax.all_to_all(jnp.stack([normed] * lax.axis_size('vocab')), 'vocab', 0, 0)]
    another operation x0 -> x1, local copies, waits for them, and re-layouts: none -> 7.25 us  [body(): jnp.stack([normed] * lax.axis_size('vocab'))]
  transfers between devices with their start and end apart: 1 -> 1, of which waited for: 1 -> 0; matrix products, arithmetic and copies ran while one was open for 1% -> 0% of each run, Pallas kernels for 0% -> 0%
where the time goes in v1:
time: 691 us; the launch traced here: 690 us
  blocking collectives  645 us (93%)
  starting transfers between devices  16.5 us (2%)
  matrix products  12 us (2%)
  other arithmetic  7.57 us (1%)
  local copies, waits for them, and re-layouts  7.55 us (1%)
    unnamed x1, blocking collectives  498 us
    pmax x1, blocking collectives, body(): top_full = lax.pmax(rowmax, 'vocab')  74.4 us
    psum x1, blocking collectives, body(): sums = lax.psum((total * factor, weighted * factor, picked), 'vocab')  73.4 us
    all_to_all x1, starting transfers between devices, body(): lax.all_to_all(jnp.stack([normed] * lax.axis_size('vocab')), 'vocab', 0, 0)  16.5 us
  transfers between devices with their start and end apart: 1, of which 0 were waited for; matrix products, arithmetic and copies ran while one was open for 0% of the time, Pallas kernels for 0%

profile of v1, /device:TPU:1, one launch (start us, length us, event | category | flops | bytes accessed | tf_op | source)
XLA Modules:
  0.0 689.9 jit_solution(3392084549813575766)
XLA Ops:
  0.6 0.0 copy-start
  0.6 1.1 fusion.2
  1.8 1.0 fusion.4
  2.8 7.2 %stack.2 = bf16[256,16,2560]{2,1,0:T(8,128)(2,1)} broadcast(bf16[16,2560]{1,0:T(8,128)(2,1)S(1)} %fusion.4), dimensions={1,2} | broadcast | bytes 21053440 | tf_op jit(solution)/shard_map/stack | solution.py:33
  10.0 0.0 copy-start.3
  10.0 0.0 copy-start.1
  10.0 0.0 copy-start.2
  10.0 16.5 %all-to-all-start = ((bf16[256,16,2560]{2,1,0:T(8,128)(2,1)}), bf16[256,16,2560]{2,1,0:T(8,128)(2,1)}, u32[]{:S(2)}, u32[]{:S(2)}) async-start(bf16[256,16,2560]{2,1,0:T(8,128)(2,1)} %stack.2), calls=%async_computation | async-start | bytes 41943040 | tf_op jit(solution)/shard_map/all_to_all | solution.py:33
  26.6 0.0 copy-done.3
  26.6 0.3 dynamic-update-slice
  26.9 497.7 %all-reduce = s32[4096]{0:T(1024)S(1)} all-reduce(s32[4096]{0:T(1024)S(1)} %dynamic-update-slice), channel_id=1, replica_groups=mesh['vocab'=256] {'vocab'}, use_global_device_ids=true, to_apply=%add | all-reduce | flops 4096 | bytes 32768
  524.6 0.0 copy-done.1
  524.6 0.0 copy-done.2
  524.6 0.6 select_reduce_fusion.2
  525.2 0.0 all-to-all-done
  525.2 0.0 copy-done
  525.2 12.0 %fusion.7 = (f32[4096]{0:T(1024)S(1)}, f32[4096,288]{0,1:T(8,128)}) fusion(bf16[4096,2560]{1,0:T(8,128)(2,1)} %bitcast, bf16[2560,288]{0,1:T(8,128)(2,1)S(1)} %copy-done, pred[288]{0:T(512)(128)(4,1)S(1)} %broadcast_compare_fusion), kind=kOutput, calls=%fused_computation.20 | convolution fusion | flops 6043332608 | bytes 27181344 | tf_op jit(solution)/shard_map/dot_general | solution.py:12
  537.2 74.4 %pmax.7 = f32[4096]{0:T(1024)S(1)} all-reduce(f32[4096]{0:T(1024)S(1)} %get-tuple-element.12), channel_id=1, replica_groups=mesh['vocab'=256] {'vocab'}, use_global_device_ids=true, to_apply=%region_5.6 | all-reduce | flops 4096 | bytes 32768 | tf_op jit(solution)/shard_map/pmax | solution.py:43
  611.6 3.7 select_reduce_fusion
  615.3 73.4 %all-reduce.1 = (f32[4096]{0:T(1024)S(1)}, f32[4096]{0:T(1024)S(1)}, f32[4096]{0:T(1024)S(1)}) all-reduce(f32[4096]{0:T(1024)S(1)} %get-tuple-element.4, f32[4096]{0:T(1024)S(1)} %get-tuple-element.11, f32[4096]{0:T(1024)S(1)} %get-tuple-element.10), channel_id=1, replica_groups=mesh['vocab'=256] {'vocab'}, use_global_device_ids=true, to_apply=%region_3.4 | all-reduce | flops 12288 | bytes 98304 | tf_op jit(solution)/shard_map/psum | solution.py:45
  688.7 1.1 compare_select_fusion
  (5 shorter events, 0.0 us)
Async XLA Ops:
  0.6 524.6 %copy-start = (bf16[2560,288]{0,1:T(8,128)(2,1)S(1)}, bf16[2560,288]{0,1:T(8,128)(2,1)}, u32[]{:S(2)}) copy-start(bf16[2560,288]{0,1:T(8,128)(2,1)} %param.8) | copy-start | bytes 4423684
  10.0 16.6 %copy-start.3 = (s32[16]{0:T(128)S(1)}, s32[16]{0:T(128)}, u32[]{:S(2)}) copy-start(s32[16]{0:T(128)} %param.9) | copy-start | bytes 196
  10.0 514.6 %copy-start.1 = (s32[512]{0:T(512)S(1)}, s32[512]{0:T(512)}, u32[]{:S(2)}) copy-start(s32[512]{0:T(512)} %param.10) | copy-start | bytes 6148
  10.0 514.6 %copy-start.2 = (s32[512]{0:T(512)S(1)}, s32[512]{0:T(512)}, u32[]{:S(2)}) copy-start(s32[512]{0:T(512)} %param.11) | copy-start | bytes 6148
  10.0 515.2 %all-to-all-start = ((bf16[256,16,2560]{2,1,0:T(8,128)(2,1)}), bf16[256,16,2560]{2,1,0:T(8,128)(2,1)}, u32[]{:S(2)}, u32[]{:S(2)}) async-start(bf16[256,16,2560]{2,1,0:T(8,128)(2,1)} %stack.2), calls=%async_computation | async-start | bytes 41943040 | tf_op jit(solution)/shard_map/all_to_all | solution.py:33
